TPU v7x, 256 devices: a whole 4x4x8 slice. The times are simulated.
256 devices in a mesh: layer: 32 (over y, z), row: 2 (over core), col: 4 (over x).
Axes of the slice: x: 4, y: 4, z: 8, core: 2. Of those that a mesh axis runs over, the one named last changes fastest.
Arguments:
- lpanel: bfloat16 [32, 8, 3072, 256], P('layer', None, 'row', 'col'), may hold values from -6 to 6
- upanel: bfloat16 [32, 8, 256, 3072], P('layer', None, 'row', 'col'), may hold values from -0.03125 to 0.03125
- lpat: int32 [32, 8, 24], P('layer', None, 'row'), may hold values 0 or 1
- upat: int32 [32, 8, 24], P('layer', None, 'col'), may hold values 0 or 1
- ancestor_entries: float32 [3072, 3072], P('row', 'col'), may hold values from -2 to 64, as said below
Outputs:
- schur: float32 [3072, 3072], P(('row', 'layer'), 'col')
- diag_lu: float32 [24, 128, 128], P('col')
Inputs may be any that keep to these rules, and one draw needn't show every extreme that they name: `ancestor_entries`: entries on the diagonal lie in 32 to 64; all other entries in -2 to 2.
All inputs are finite; a program needn't handle non-finite values. No bound on the sum of `lpat` or of `upat` on one device may be relied on, other than what follows from the above.
Results may differ from a plain program's by a relative error of at most 0.0003.
Values may be sent and summed in bfloat16 or wider, within the bound.
A program may use at most 64 MiB of HBM per device.

v0:
```python
import jax
import jax.numpy as jnp
from jax import lax
from jax.sharding import PartitionSpec as P

BLK = 128
panel_width = 16


def mask_rows(panel, pattern, block):
    count, length, inner = panel.shape
    shaped = panel.reshape(count, length // block, block, inner)
    return (shaped * pattern[:, :, None, None].astype(panel.dtype)).reshape(count, length, inner)


def mask_cols(panel, pattern, block):
    count, inner, length = panel.shape
    shaped = panel.reshape(count, inner, length // block, block)
    return (shaped * pattern[:, None, :, None].astype(panel.dtype)).reshape(count, inner, length)


def eliminate_tall(tile, steps):
    row_places = jnp.arange(tile.shape[1])
    col_places = jnp.arange(tile.shape[2])

    def eliminate_sweep(step, current):
        pivot = current[:, step, step]
        below = row_places > step
        column = jnp.where(below[None, :], current[:, :, step] / pivot[:, None], 0.0)
        right = col_places > step
        row_part = jnp.where(right[None, :], current[:, step, :], 0.0)
        current = current - column[:, :, None] * row_part[:, None, :]
        placed = below[None, :, None] & (col_places == step)[None, None, :]
        return jnp.where(placed, column[:, :, None], current)

    return lax.fori_loop(0, steps, eliminate_sweep, tile)


def forward_rows(unit, strip):
    places = jnp.arange(unit.shape[1])

    def forward_sweep(step, current):
        factors = jnp.where(places[None, :] > step, unit[:, :, step], 0.0)
        return current - factors[:, :, None] * current[:, step, :][:, None, :]

    return lax.fori_loop(0, unit.shape[1], forward_sweep, strip)


def factor(blocks):
    size = blocks.shape[-1]
    current = blocks
    for offset in range(0, size, panel_width):
        end = offset + panel_width
        panel = eliminate_tall(current[:, offset:, offset:end], panel_width)
        current = current.at[:, offset:, offset:end].set(panel)
        if end < size:
            strip = forward_rows(panel[:, :panel_width, :], current[:, offset:end, end:])
            current = current.at[:, offset:end, end:].set(strip)
            lower = panel[:, panel_width:, :]
            trailing = current[:, end:, end:] - jnp.einsum(
                "bik,bkj->bij",
                lower,
                strip,
                precision=lax.Precision.HIGHEST,
                preferred_element_type=jnp.float32,
            )
            current = current.at[:, end:, end:].set(trailing)
    return current


def candidates(matrix):
    width = matrix.shape[1]
    per_group = lax.axis_size("col") // lax.axis_size("row")
    column = lax.axis_index("col")
    valid = column // per_group == lax.axis_index("row")
    begin = column % per_group * width
    square = lax.dynamic_slice_in_dim(matrix, begin, width, 0)
    count = width // BLK
    blocks = jnp.stack(
        [square[j * BLK : (j + 1) * BLK, j * BLK : (j + 1) * BLK] for j in range(count)]
    )
    return (blocks, valid)


def pick_owned(gathered):
    per_group = lax.axis_size("col") // lax.axis_size("row")
    count = gathered.shape[0] // lax.axis_size("row")
    source = lax.axis_index("col") // per_group
    return lax.dynamic_slice_in_dim(gathered, source * count, count, 0)


def shards(lpanel, upanel, lpat, upat, ancestor_entries):
    left_masked = mask_rows(lpanel[0], lpat[0], BLK)
    right_masked = mask_cols(upanel[0], upat[0], BLK)
    right_full = lax.all_gather(right_masked, "row", axis=1, tiled=True)
    length = left_masked.shape[1]
    update = jnp.einsum(
        "kmw,kwn->mn",
        lax.all_gather(left_masked, "col", axis=2, tiled=True),
        right_full,
        preferred_element_type=jnp.float32,
    )
    share_rows = length // lax.axis_size("layer")
    offset = lax.axis_index("layer") * share_rows
    total = lax.psum(update, "layer")
    summed = ancestor_entries - total
    schur = lax.dynamic_slice_in_dim(summed, offset, share_rows, 0)
    pivots, valid = candidates(summed)
    diag_lu = factor(pick_owned(lax.all_gather(pivots, "row", axis=0, tiled=True)))
    return (schur, diag_lu)


def solution(mesh):
    return jax.shard_map(
        shards,
        mesh=mesh,
        in_specs=(
            P("layer", None, "row", "col"),
            P("layer", None, "row", "col"),
            P("layer", None, "row"),
            P("layer", None, "col"),
            P("row", "col"),
        ),
        out_specs=(P(("row", "layer"), "col"), P("col", None, None)),
        check_vma=False,
    )
```

profile of v0, /device:TPU:1, one launch (start us, length us, event | category | flops | bytes accessed | tf_op | source)
XLA Modules:
  0.0 484.4 jit_solution(14656002472003928525)
XLA Ops:
  7.2 0.9 copy.122
  8.3 2.7 bitcast_multiply_fusion
  11.2 1.4 bitcast_multiply_fusion.1
  12.6 20.4 %all-gather.5.cloned.1.call-done = bf16[8,256,768]{2,1,0:T(8,128)(2,1)} async-done(((bf16[8,128,768]{2,1,0:T(8,128)(2,1)}), bf16[8,256,768]{2,1,0:T(8,128)(2,1)}) %all-gather.5.cloned.1.call-update) | async-done | bytes 3145744 | tf_op jit(solution)/shard_map/all_gather | solution.py:95
  33.1 70.4 %all-gather.3.cloned.1.call-done = bf16[8,1536,256]{1,2,0:T(8,128)(2,1)} async-done(((bf16[8,1536,64]{1,2,0:T(8,128)(2,1)}), bf16[8,1536,256]{1,2,0:T(8,128)(2,1)}) %all-gather.3.cloned.1.call-update) | async-done | bytes 6291472 | tf_op jit(solution)/shard_map/all_gather | solution.py:99
  103.5 9.7 %convolution_bitcast_fusion = f32[1536,768]{1,0:T(8,128)} fusion(bf16[8,1536,256]{1,2,0:T(8,128)(2,1)} %all-gather.3.cloned.1.call-done, bf16[8,256,768]{2,1,0:T(8,128)(2,1)} %all-gather.5.cloned.1.call-done), kind=kOutput, calls=%fused_computation.119 | convolution fusion | flops 4831838208 | bytes 14155776 | tf_op jit(solution)/shard_map/kmw,kwn->mn/dot_general | solution.py:97
  114.6 166.0 %all-reduce.2.cloned.1.call-done = f32[1536,768]{1,0:T(8,128)} async-done(((f32[1536,768]{1,0:T(8,128)}), f32[1536,768]{1,0:T(8,128)}) %all-reduce.2.cloned.1.call-update) | async-done | bytes 4718608 | tf_op jit(solution)/shard_map/psum | solution.py:105
  280.6 4.4 sub.134
  285.1 3.9 all_gather.11
  289.3 13.2 %while.248 = (s32[]{:T(128)}, f32[6,128,16]{1,0,2:T(8,128)S(1)}, s32[]{:T(128)}) while((s32[]{:T(128)}, f32[6,128,16]{1,0,2:T(8,128)S(1)}, s32[]{:T(128)}) %tuple.580), condition=%wide.region_2.3_spmd.clone.clone, body=%wide.region_1.2_spmd.clone.clone.sunk | while | flops 40706 | bytes 212433 | solution.py:36
  302.6 2.6 while.241
  305.4 2.1 dynamic-slice_select_fusion
  307.4 6.4 %scatter.75 = f32[6,128,128]{1,2,0:T(8,128)S(1)} dynamic-update-slice(f32[6,128,128]{1,2,0:T(8,128)S(1)} %get-tuple-element.1863, f32[6,16,112]{1,2,0:T(8,128)S(1)} %dynamic-slice_select_fusion, s32[]{:T(128)} %constant.1116.clone.1, s32[]{:T(128)} %bitcast.13, s32[]{:T(128)} %bitcast.14) | dynamic-update-slice | bytes 86020 | tf_op jit(solution)/shard_map/scatter | solution.py:58
  314.6 7.3 %scatter.76 = f32[6,128,128]{1,2,0:T(8,128)S(1)} dynamic-update-slice(f32[6,128,128]{1,2,0:T(8,128)S(1)} %scatter.75, f32[6,112,112]{1,2,0:T(8,128)S(1)} %convolution_subtract_fusion, s32[]{:T(128)} %constant.1116.clone.1, s32[]{:T(128)} %constant.1125.clone.1, s32[]{:T(128)} %constant.1125.clone.1) | dynamic-update-slice | bytes 602116 | tf_op jit(solution)/shard_map/scatter | solution.py:67
  322.0 12.9 %while.249 = (s32[]{:T(128)}, f32[6,112,16]{1,0,2:T(8,128)S(1)}, s32[]{:T(128)}) while((s32[]{:T(128)}, f32[6,112,16]{1,0,2:T(8,128)S(1)}, s32[]{:T(128)}) %tuple.586), condition=%wide.region_7.8_spmd.clone.clone, body=%wide.region_6.7_spmd.clone.clone.sunk | while | flops 35634 | bytes 186145 | solution.py:36
  334.9 2.3 scatter.79
  337.4 2.5 while.242
  340.1 3.2 scatter.80
  344.0 3.2 scatter.81
  347.3 12.5 %while.250 = (s32[]{:T(128)}, f32[6,96,16]{1,0,2:T(8,128)S(1)}, s32[]{:T(128)}) while((s32[]{:T(128)}, f32[6,96,16]{1,0,2:T(8,128)S(1)}, s32[]{:T(128)}) %tuple.592), condition=%wide.region_11.12_spmd.clone.clone, body=%wide.region_10.11_spmd.clone.clone.sunk | while | flops 30562 | bytes 159857 | solution.py:36
  359.9 2.3 scatter.84
  362.4 2.6 while.243
  365.1 3.0 scatter.85
  368.7 3.0 scatter.86
  371.8 12.1 %while.251 = (s32[]{:T(128)}, f32[6,80,16]{1,0,2:T(8,128)S(1)}, s32[]{:T(128)}) while((s32[]{:T(128)}, f32[6,80,16]{1,0,2:T(8,128)S(1)}, s32[]{:T(128)}) %tuple.598), condition=%wide.region_15.16_spmd.clone.clone, body=%wide.region_14.15_spmd.clone.clone.sunk | while | flops 25490 | bytes 133569 | solution.py:36
  383.9 2.3 scatter.89
  386.4 2.5 while.244
  389.1 3.0 scatter.90
  392.7 2.8 scatter.91
  395.6 11.8 %while.252 = (s32[]{:T(128)}, f32[6,64,16]{1,0,2:T(8,128)S(1)}, s32[]{:T(128)}) while((s32[]{:T(128)}, f32[6,64,16]{1,0,2:T(8,128)S(1)}, s32[]{:T(128)}) %tuple.604), condition=%wide.region_19.20_spmd.clone.clone, body=%wide.region_18.19_spmd.clone.clone.sunk | while | flops 20418 | bytes 107281 | solution.py:36
  407.4 2.3 scatter.94
  409.8 2.5 while.245
  412.5 2.6 scatter.95
  415.6 2.6 scatter.96
  418.3 11.5 %while.253 = (s32[]{:T(128)}, f32[6,48,16]{1,0,2:T(8,128)S(1)}, s32[]{:T(128)}) while((s32[]{:T(128)}, f32[6,48,16]{1,0,2:T(8,128)S(1)}, s32[]{:T(128)}) %tuple.610), condition=%wide.region_23.24_spmd.clone.clone, body=%wide.region_22.23_spmd.clone.clone.sunk | while | flops 15346 | bytes 80993 | solution.py:36
  429.8 2.3 scatter.99
  432.3 2.5 while.246
  434.9 2.4 scatter.100
  437.8 2.4 scatter.101
  440.2 11.1 %while.254 = (s32[]{:T(128)}, f32[6,32,16]{1,0,2:T(8,128)S(1)}, s32[]{:T(128)}) while((s32[]{:T(128)}, f32[6,32,16]{1,0,2:T(8,128)S(1)}, s32[]{:T(128)}) %tuple.616), condition=%wide.region_27.28_spmd.clone.clone, body=%wide.region_26.27_spmd.clone.clone.sunk | while | flops 10274 | bytes 54705 | solution.py:36
  451.5 2.3 scatter.104
  454.0 3.8 while.247
  457.8 2.2 scatter.105
  460.2 2.2 scatter.106
  462.5 1.6 constant_dynamic-slice_fusion.7
  464.0 10.7 %while.255 = (s32[]{:T(128)}, f32[6,16,16]{1,0,2:T(8,128)S(1)}, s32[]{:T(128)}) while((s32[]{:T(128)}, f32[6,16,16]{1,0,2:T(8,128)S(1)}, s32[]{:T(128)}) %tuple.622), condition=%wide.region_31.32_spmd.clone.clone, body=%wide.region_30.31_spmd.clone.clone.sunk | while | flops 5186 | bytes 28397 | solution.py:36
  474.8 2.2 scatter.109
  477.0 0.9 copy.164
  (1779 shorter events, 111.6 us)
Async XLA Ops:
  7.2 3.8 copy-start.2
  7.2 4.0 copy-start.1
  7.2 25.9 %all-gather.5.cloned.1.call-start = ((), (), s32[]{:S(2)}) async-start(), calls=%async_computation.1 | async-start | bytes 4718592 | tf_op jit(solution)/shard_map/all_gather | solution.py:95
  11.0 92.5 %all-gather.3.cloned.1.call-start = ((), (), s32[]{:S(2)}) async-start(), calls=%async_computation | async-start | bytes 7864320 | tf_op jit(solution)/shard_map/all_gather | solution.py:99
  12.6 268.0 %all-reduce.2.cloned.1.call-start = ((), (), s32[]{:S(2)}) async-start(), calls=%async_computation.2 | async-start | bytes 9437184 | tf_op jit(solution)/shard_map/psum | solution.py:105
  113.2 0.7 copy-start.3
  285.0 4.1 copy-start
Sparse Core Ops, SparseCore 0:
  11.1 21.9 all-gather.4
  34.9 68.5 all-gather.2
  113.3 167.2 all-reduce.1
where the time goes:
time: 485 us; the launch traced here: 484 us
  waiting for transfers between devices  257 us (53%)
  local copies, waits for them, and re-layouts  128 us (26%)
  other arithmetic  55.7 us (11%)
  between operations  14.5 us (3%)
  matrix products  13.4 us (3%)
  loops' own time  11.6 us (2%)
    psum x1, waiting for transfers between devices, shards(): total = lax.psum(update, 'layer')  166 us
    all_gather x1, waiting for transfers between devices, shards(): lax.all_gather(left_masked, 'col', axis=2, tiled=True)  70.4 us
    scatter x7, local copies, waits for them, and re-layouts, factor(): current = current.at[:, end:, end:].set(trailing)  23.7 us
    dynamic_slice x128, local copies, waits for them, and re-layouts, eliminate_sweep(): pivot = current[:, step, step]  23.6 us
    scatter x7, local copies, waits for them, and re-layouts, factor(): current = current.at[:, offset:end, end:].set(strip)  22.9 us
    while x224, local copies, waits for them, and re-layouts  22 us
    all_gather x1, waiting for transfers between devices, shards(): right_full = lax.all_gather(right_masked, 'row', axis=1, tiled=True)  20.4 us
    scatter x8, local copies, waits for them, and re-layouts, factor(): current = current.at[:, offset:, offset:end].set(panel)  16 us
  transfers between devices with their start and end apart: 3, of which 3 were waited for; matrix products, arithmetic and copies ran while one was open for 1% of the time, Pallas kernels for 0%

commit v1 on v0

--- a/solution.py
+++ b/solution.py
@@ -102,7 +102,9 @@
     )
     share_rows = length // lax.axis_size("layer")
     offset = lax.axis_index("layer") * share_rows
-    total = lax.psum(update, "layer")
+    total = update
+    for hop in (1, 2, 4, 8, 16):
+        total = total + lax.ppermute(total, "layer", [(dev, dev ^ hop) for dev in range(32)])
     summed = ancestor_entries - total
     schur = lax.dynamic_slice_in_dim(summed, offset, share_rows, 0)
     pivots, valid = candidates(summed)

time: 485 us -> 1050 us (2.16)
  waiting for transfers between devices: 257 us -> 798 us
  starting transfers between devices: 0.12 us -> 14.3 us
    ppermute x0 -> x5, waiting for transfers between devices: none -> 707 us  [shards(): lax.ppermute(total, 'layer', [(dev, dev ^ hop) for dev in range(32)])]
    psum x1 -> x0, waiting for transfers between devices: 166 us -> none  [shards(): total = lax.psum(update, 'layer')]
    ppermute x0 -> x5, starting transfers between devices: none -> 14.2 us  [shards(): lax.ppermute(total, 'layer', [(dev, dev ^ hop) for dev in range(32)])]
  transfers between devices with their start and end apart: 3 -> 7, of which waited for: 3 -> 7; matrix products, arithmetic and copies ran while one was open for 1% -> 0% of each run, Pallas kernels for 0% -> 0%
where the time goes in v1:
time: 1050 us
  waiting for transfers between devices  798 us (76%)
  local copies, waits for them, and re-layouts  128 us (12%)
  other arithmetic  61.9 us (6%)
  between operations  14.8 us (1%)
  starting transfers between devices  14.3 us (1%)
  matrix products  12 us (1%)
  loops' own time  11.6 us (1%)
    ppermute x5, waiting for transfers between devices, shards(): lax.ppermute(total, 'layer', [(dev, dev ^ hop) for dev in range(32)])  707 us
    all_gather x1, waiting for transfers between devices, shards(): lax.all_gather(left_masked, 'col', axis=2, tiled=True)  70.4 us
    scatter x7, local copies, waits for them, and re-layouts, factor(): current = current.at[:, end:, end:].set(trailing)  23.7 us
    dynamic_slice x128, local copies, waits for them, and re-layouts, eliminate_sweep(): pivot = current[:, step, step]  23.6 us
    scatter x7, local copies, waits for them, and re-layouts, factor(): current = current.at[:, offset:end, end:].set(strip)  22.9 us
    while x224, local copies, waits for them, and re-layouts  22 us
  transfers between devices with their start and end apart: 7, of which 7 were waited for; matrix products, arithmetic and copies ran while one was open for 0% of the time, Pallas kernels for 0%

profile of v1, /device:TPU:1, one launch (start us, length us, event | category | flops | bytes accessed | tf_op | source)
XLA Modules:
  0.0 1045.8 jit_solution(8522815536300240366)
XLA Ops:
  8.3 2.7 bitcast_multiply_fusion
  12.5 20.6 %all-gather.5.cloned.1.call-done = bf16[8,256,768]{2,1,0:T(8,128)(2,1)} async-done(((bf16[8,128,768]{2,1,0:T(8,128)(2,1)}), bf16[8,256,768]{2,1,0:T(8,128)(2,1)}) %all-gather.5.cloned.1.call-update) | async-done | bytes 3145744 | tf_op jit(solution)/shard_map/all_gather | solution.py:95
  33.1 70.4 %all-gather.3.cloned.1.call-done = bf16[8,1536,256]{1,2,0:T(8,128)(2,1)} async-done(((bf16[8,1536,64]{1,2,0:T(8,128)(2,1)}), bf16[8,1536,256]{1,2,0:T(8,128)(2,1)}) %all-gather.3.cloned.1.call-update) | async-done | bytes 6291472 | tf_op jit(solution)/shard_map/all_gather | solution.py:99
  103.5 8.3 convolution_bitcast_fusion
  113.2 101.2 %collective-permute-done = f32[1536,768]{1,0:T(8,128)S(1)} collective-permute-done((f32[1536,768]{1,0:T(8,128)S(1)}, f32[1536,768]{1,0:T(8,128)S(1)}, u32[]{:S(2)}, u32[]{:S(2)}) %collective-permute-start) | collective-permute-done | bytes 4718624 | tf_op jit(solution)/shard_map/ppermute | solution.py:107
  215.0 2.4 collective-permute-start.1
  217.4 202.5 %collective-permute-done.1 = f32[1536,768]{1,0:T(8,128)S(1)} collective-permute-done((f32[1536,768]{1,0:T(8,128)S(1)}, f32[1536,768]{1,0:T(8,128)S(1)}, u32[]{:S(2)}, u32[]{:S(2)}) %collective-permute-start.1) | collective-permute-done | bytes 4718624 | tf_op jit(solution)/shard_map/ppermute | solution.py:107
  420.4 6.4 collective-permute-start.2
  426.9 203.5 %collective-permute-done.2 = f32[1536,768]{1,0:T(8,128)S(1)} collective-permute-done((f32[1536,768]{1,0:T(8,128)S(1)}, f32[1536,768]{1,0:T(8,128)S(1)}, u32[]{:S(2)}, u32[]{:S(2)}) %collective-permute-start.2) | collective-permute-done | bytes 4718624 | tf_op jit(solution)/shard_map/ppermute | solution.py:107
  632.2 100.8 %collective-permute-done.3 = f32[1536,768]{1,0:T(8,128)S(1)} collective-permute-done((f32[1536,768]{1,0:T(8,128)S(1)}, f32[1536,768]{1,0:T(8,128)S(1)}, u32[]{:S(2)}, u32[]{:S(2)}) %collective-permute-start.3) | collective-permute-done | bytes 4718624 | tf_op jit(solution)/shard_map/ppermute | solution.py:107
  733.0 2.7 add.456
  735.7 2.7 collective-permute-start.4
  739.9 98.7 %collective-permute-done.4 = f32[1536,768]{1,0:T(8,128)} collective-permute-done((f32[1536,768]{1,0:T(8,128)}, f32[1536,768]{1,0:T(8,128)}, u32[]{:S(2)}, u32[]{:S(2)}) %collective-permute-start.4) | collective-permute-done | bytes 4718624 | tf_op jit(solution)/shard_map/ppermute | solution.py:107
  838.6 6.0 add_subtract_fusion
  844.8 5.3 all_gather.11
  850.3 13.2 %while.248 = (s32[]{:T(128)}, f32[6,128,16]{1,0,2:T(8,128)S(1)}, s32[]{:T(128)}) while((s32[]{:T(128)}, f32[6,128,16]{1,0,2:T(8,128)S(1)}, s32[]{:T(128)}) %tuple.580), condition=%wide.region_1.2_spmd.clone.clone, body=%wide.region_0.1_spmd.clone.clone.sunk | while | flops 40706 | bytes 212433 | solution.py:36
  863.7 2.6 while.241
  868.5 6.4 scatter.75
  875.7 7.3 scatter.76
  883.1 12.9 %while.249 = (s32[]{:T(128)}, f32[6,112,16]{1,0,2:T(8,128)S(1)}, s32[]{:T(128)}) while((s32[]{:T(128)}, f32[6,112,16]{1,0,2:T(8,128)S(1)}, s32[]{:T(128)}) %tuple.586), condition=%wide.region_6.7_spmd.clone.clone, body=%wide.region_5.6_spmd.clone.clone.sunk | while | flops 35634 | bytes 186145 | solution.py:36
  896.0 2.3 scatter.79
  898.5 2.5 while.242
  901.2 3.2 scatter.80
  905.1 3.2 scatter.81
  908.4 12.5 %while.250 = (s32[]{:T(128)}, f32[6,96,16]{1,0,2:T(8,128)S(1)}, s32[]{:T(128)}) while((s32[]{:T(128)}, f32[6,96,16]{1,0,2:T(8,128)S(1)}, s32[]{:T(128)}) %tuple.592), condition=%wide.region_10.11_spmd.clone.clone, body=%wide.region_9.10_spmd.clone.clone.sunk | while | flops 30562 | bytes 159857 | solution.py:36
  920.9 2.3 scatter.84
  923.5 2.6 while.243
  926.1 3.0 scatter.85
  929.8 3.0 scatter.86
  932.9 12.1 %while.251 = (s32[]{:T(128)}, f32[6,80,16]{1,0,2:T(8,128)S(1)}, s32[]{:T(128)}) while((s32[]{:T(128)}, f32[6,80,16]{1,0,2:T(8,128)S(1)}, s32[]{:T(128)}) %tuple.598), condition=%wide.region_14.15_spmd.clone.clone, body=%wide.region_13.14_spmd.clone.clone.sunk | while | flops 25490 | bytes 133569 | solution.py:36
  945.0 2.3 scatter.89
  947.5 2.5 while.244
  950.2 3.0 scatter.90
  953.8 2.8 scatter.91
  956.6 11.8 %while.252 = (s32[]{:T(128)}, f32[6,64,16]{1,0,2:T(8,128)S(1)}, s32[]{:T(128)}) while((s32[]{:T(128)}, f32[6,64,16]{1,0,2:T(8,128)S(1)}, s32[]{:T(128)}) %tuple.604), condition=%wide.region_18.19_spmd.clone.clone, body=%wide.region_17.18_spmd.clone.clone.sunk | while | flops 20418 | bytes 107281 | solution.py:36
  968.5 2.3 scatter.94
  970.9 2.5 while.245
  973.6 2.6 scatter.95
  976.7 2.6 scatter.96
  979.4 11.5 %while.253 = (s32[]{:T(128)}, f32[6,48,16]{1,0,2:T(8,128)S(1)}, s32[]{:T(128)}) while((s32[]{:T(128)}, f32[6,48,16]{1,0,2:T(8,128)S(1)}, s32[]{:T(128)}) %tuple.610), condition=%wide.region_22.23_spmd.clone.clone, body=%wide.region_21.22_spmd.clone.clone.sunk | while | flops 15346 | bytes 80993 | solution.py:36
  990.9 2.3 scatter.99
  993.3 2.5 while.246
  996.0 2.4 scatter.100
  998.8 2.4 scatter.101
  1001.3 11.1 %while.254 = (s32[]{:T(128)}, f32[6,32,16]{1,0,2:T(8,128)S(1)}, s32[]{:T(128)}) while((s32[]{:T(128)}, f32[6,32,16]{1,0,2:T(8,128)S(1)}, s32[]{:T(128)}) %tuple.616), condition=%wide.region_26.27_spmd.clone.clone, body=%wide.region_25.26_spmd.clone.clone.sunk | while | flops 10274 | bytes 54705 | solution.py:36
  1012.6 2.3 scatter.104
  1015.0 3.8 while.247
  1025.1 10.7 %while.255 = (s32[]{:T(128)}, f32[6,16,16]{1,0,2:T(8,128)S(1)}, s32[]{:T(128)}) while((s32[]{:T(128)}, f32[6,16,16]{1,0,2:T(8,128)S(1)}, s32[]{:T(128)}) %tuple.622), condition=%wide.region_30.31_spmd.clone.clone, body=%wide.region_29.30_spmd.clone.clone.sunk | while | flops 5186 | bytes 28397 | solution.py:36
  (1790 shorter events, 129.4 us)
Async XLA Ops:
  7.2 3.9 copy-start.2
  7.2 4.1 copy-start.1
  7.2 25.9 %all-gather.5.cloned.1.call-start = ((), (), s32[]{:S(2)}) async-start(), calls=%async_computation.1 | async-start | bytes 4718592 | tf_op jit(solution)/shard_map/all_gather | solution.py:95
  11.0 92.5 %all-gather.3.cloned.1.call-start = ((), (), s32[]{:S(2)}) async-start(), calls=%async_computation | async-start | bytes 7864320 | tf_op jit(solution)/shard_map/all_gather | solution.py:99
  111.8 102.6 %collective-permute-start = (f32[1536,768]{1,0:T(8,128)S(1)}, f32[1536,768]{1,0:T(8,128)S(1)}, u32[]{:S(2)}, u32[]{:S(2)}) collective-permute-start(f32[1536,768]{1,0:T(8,128)S(1)} %convolution_bitcast_fusion), channel_id=1, source_target_pairs={{0,8},{8,0},{16,24},{24,16},{32,40},{40,32},{48,56},{56,48},{64,72... | collective-permute-start | bytes 14155784 | tf_op jit(solution)/shard_map/ppermute | solution.py:107
  215.0 204.8 %collective-permute-start.1 = (f32[1536,768]{1,0:T(8,128)S(1)}, f32[1536,768]{1,0:T(8,128)S(1)}, u32[]{:S(2)}, u32[]{:S(2)}) collective-permute-start(f32[1536,768]{1,0:T(8,128)S(1)} %add.453), channel_id=1, source_target_pairs={{0,16},{8,24},{16,0},{24,8},{32,48},{40,56},{48,32},{56,40},{64,80... | collective-permute-start | bytes 14155784 | tf_op jit(solution)/shard_map/ppermute | solution.py:107
  420.4 209.9 %collective-permute-start.2 = (f32[1536,768]{1,0:T(8,128)S(1)}, f32[1536,768]{1,0:T(8,128)S(1)}, u32[]{:S(2)}, u32[]{:S(2)}) collective-permute-start(f32[1536,768]{1,0:T(8,128)S(1)} %add.454), channel_id=1, source_target_pairs={{0,32},{8,40},{16,48},{24,56},{32,0},{40,8},{48,16},{56,24},{64,96... | collective-permute-start | bytes 14155784 | tf_op jit(solution)/shard_map/ppermute | solution.py:107
  630.9 108.2 %copy-start.3 = (s32[3]{0:T(128)S(1)}, s32[3]{0:T(128)}, u32[]{:S(2)}) copy-start(s32[3]{0:T(128)} %constant.1126.clone.1) | copy-start | bytes 40
  630.9 102.0 %collective-permute-start.3 = (f32[1536,768]{1,0:T(8,128)S(1)}, f32[1536,768]{1,0:T(8,128)S(1)}, u32[]{:S(2)}, u32[]{:S(2)}) collective-permute-start(f32[1536,768]{1,0:T(8,128)S(1)} %add.455), channel_id=1, source_target_pairs={{0,64},{8,72},{16,80},{24,88},{32,96},{40,104},{48,112},{56,120},{... | collective-permute-start | bytes 14155784 | tf_op jit(solution)/shard_map/ppermute | solution.py:107
  735.7 102.9 %collective-permute-start.4 = (f32[1536,768]{1,0:T(8,128)}, f32[1536,768]{1,0:T(8,128)}, u32[]{:S(2)}, u32[]{:S(2)}) collective-permute-start(f32[1536,768]{1,0:T(8,128)} %add.456), channel_id=1, source_target_pairs={{0,128},{8,136},{16,144},{24,152},{32,160},{40,168},{48,176},{56,1... | collective-permute-start | bytes 14155784 | tf_op jit(solution)/shard_map/ppermute | solution.py:107
  844.6 5.5 copy-start
Sparse Core Ops, SparseCore 0:
  11.1 21.9 all-gather.4
  34.9 68.5 all-gather.2
